TPU v7x, 512 devices: a whole 4x8x8 slice. The times are simulated.
512 devices in a mesh: wide: 64 (over z, y_hi, core), narrow: 8 (over x, y_lo).
Axes of the slice: x: 4, y: 8 (y_hi: 4, y_lo: 2; y = y_hi * 2 + y_lo), z: 8, core: 2. Of those that a mesh axis runs over, the one named last changes fastest.
Arguments:
- hidden_in: bfloat16 [16384, 2048], P('wide', 'narrow'), may hold values from -64 to 64
- cache_lengths: int32 [128], P('wide'), may hold values from 1 to 1023, as said below
- cache_offsets: int32 [128], P('wide'), may hold values from 0 to 65535, as said below
- cache_kv: bfloat16 [2, 2, 65536, 2048], P(None, None, 'wide', 'narrow'), may hold values from -16 to 16
- w_qkv: bfloat16 [2048, 3, 2048], P('wide', None, 'narrow'), may hold values from -0.125 to 0.125
- qkv_bias: bfloat16 [3, 2048], P(None, 'narrow'), may hold values from -40 to 40
- w_out: bfloat16 [2048, 2048], P('wide', 'narrow'), may hold values from -0.125 to 0.125
- out_bias: bfloat16 [2048], P('narrow'), may hold values from -3 to 3
- norm_gain: bfloat16 [2048], P('narrow'), may hold values from 0.2 to 5
- norm_shift: bfloat16 [2048], P('narrow'), may hold values from -3 to 3
Outputs:
- hidden_out: bfloat16 [16384, 2048], P('wide', 'narrow')
- new_cache: bfloat16 [2, 2, 16384, 2048], P(None, None, 'wide', 'narrow')
Inputs may be any that keep to these rules, and one draw needn't show every extreme that they name: `cache_lengths`: the cached lengths of the 2 requests r with the same r // 2 sum to at most 1024; for some such group exactly 1024, and in it one request has 1023 rows. Request r's cache is rows cache_offsets[r] to cache_offsets[r] + cache_lengths[r] - 1 of the packed cache, all within rows (r // 2) * 1024 to (r // 2 + 1) * 1024 - 1; the row ranges of different requests are disjoint.
All inputs are finite; a program needn't handle non-finite values.
Results may differ from a plain program's by a relative error of at most 0.02.
Values may be sent and summed in bfloat16 or wider, within the bound.
No kernel may reach another device: no remote copies, remote signals or barrier semaphores. Data moves between devices by JAX's collectives and lax.ppermute only.
A program may use at most 64 MiB of HBM per device.

v0:
```python
import math
import jax
import jax.numpy as jnp
from jax import lax
from jax.sharding import PartitionSpec as P

HEAD = 128
SPAN = 128
LAYERS = 2
EPSILON = 1e-05
NEGATIVE = -1e30


def add_rows(shard_piece, operand):
    piece_rows = shard_piece.shape[0]
    return jnp.dot(operand, shard_piece.reshape(piece_rows, -1), preferred_element_type=jnp.float32)


def norm_slice(summed, norm_gain, norm_shift, full_width):
    values = summed.astype(jnp.float32)
    row_means = lax.psum(jnp.sum(values, axis=1), "narrow") / full_width
    centered = values - row_means[:, None]
    row_spread = lax.psum(jnp.sum(centered * centered, axis=1), "narrow") / full_width
    scaled = centered * lax.rsqrt(row_spread[:, None] + EPSILON)
    return (scaled * norm_gain.astype(jnp.float32) + norm_shift.astype(jnp.float32)).astype(
        jnp.bfloat16
    )


def attend(queries, keys_new, values_new, keys_cache, values_cache, live_cache, live_new):
    scale_factor = 1.0 / math.sqrt(queries.shape[2])
    scores_cache = (
        jnp.einsum("qhd,khd->hqk", queries, keys_cache, preferred_element_type=jnp.float32)
        * scale_factor
    )
    scores_new = (
        jnp.einsum("qhd,khd->hqk", queries, keys_new, preferred_element_type=jnp.float32)
        * scale_factor
    )
    masked_cache = jnp.where(live_cache[None], scores_cache, NEGATIVE)
    masked_new = jnp.where(live_new[None], scores_new, NEGATIVE)
    top_score = jnp.maximum(jnp.max(masked_cache, axis=2), jnp.max(masked_new, axis=2))[:, :, None]
    weights_cache = jnp.where(live_cache[None], jnp.exp(masked_cache - top_score), 0.0)
    weights_new = jnp.where(live_new[None], jnp.exp(masked_new - top_score), 0.0)
    totals = jnp.sum(weights_cache, axis=2, keepdims=True) + jnp.sum(
        weights_new, axis=2, keepdims=True
    )
    probs_cache = (weights_cache / totals).astype(jnp.bfloat16)
    probs_new = (weights_new / totals).astype(jnp.bfloat16)
    combined = jnp.einsum(
        "hqk,khd->qhd", probs_cache, values_cache, preferred_element_type=jnp.float32
    )
    combined = combined + jnp.einsum(
        "hqk,khd->qhd", probs_new, values_new, preferred_element_type=jnp.float32
    )
    return combined.astype(jnp.bfloat16).reshape(queries.shape[0], -1)


def shards(
    hidden_in,
    cache_lengths,
    cache_offsets,
    cache_kv,
    w_qkv,
    qkv_bias,
    w_out,
    out_bias,
    norm_gain,
    norm_shift,
):
    row_count, local_width = hidden_in.shape
    full_width = local_width * lax.axis_size("narrow")
    local_heads = local_width // HEAD
    cache_count = cache_kv.shape[2]
    requests_here = cache_lengths.shape[0]
    block_start = lax.axis_index("wide") * cache_count
    rows_global = block_start + jnp.arange(cache_count, dtype=jnp.int32)
    row_start = jnp.broadcast_to(cache_offsets[:, None], (requests_here, SPAN)).reshape(-1)
    row_stop = row_start + jnp.broadcast_to(cache_lengths[:, None], (requests_here, SPAN)).reshape(
        -1
    )
    live_cache = (rows_global[None, :] >= row_start[:, None]) & (
        rows_global[None, :] < row_stop[:, None]
    )
    owner_index = jnp.arange(row_count, dtype=jnp.int32) // SPAN
    position = jnp.arange(row_count, dtype=jnp.int32) % SPAN
    live_new = (owner_index[:, None] == owner_index[None, :]) & (
        position[:, None] >= position[None, :]
    )
    bias_flat = qkv_bias.astype(jnp.float32).reshape(-1)
    gathered = lax.all_gather(hidden_in, "narrow", axis=1, tiled=True)
    carried = hidden_in
    appended = []
    for layer_index in range(LAYERS):
        projections = add_rows(lax.all_gather(w_qkv, "wide", axis=0, tiled=True), operand=gathered)
        projections = projections + bias_flat
        queries = projections[:, :local_width].astype(jnp.bfloat16)
        keys_new = projections[:, local_width : 2 * local_width].astype(jnp.bfloat16)
        values_new = projections[:, 2 * local_width :].astype(jnp.bfloat16)
        appended.append(jnp.stack([keys_new, values_new]))
        keys_cache = cache_kv[layer_index, 0].reshape(cache_count, local_heads, HEAD)
        values_cache = cache_kv[layer_index, 1].reshape(cache_count, local_heads, HEAD)
        attended = attend(
            queries.reshape(row_count, local_heads, HEAD),
            keys_new.reshape(row_count, local_heads, HEAD),
            values_new.reshape(row_count, local_heads, HEAD),
            keys_cache,
            values_cache,
            live_cache,
            live_new,
        )
        heads_all = lax.all_gather(attended, "narrow", axis=1, tiled=True)
        projected = add_rows(lax.all_gather(w_out, "wide", axis=0, tiled=True), operand=heads_all)
        summed = (projected + out_bias.astype(jnp.float32) + carried.astype(jnp.float32)).astype(
            jnp.bfloat16
        )
        if layer_index + 1 < LAYERS:
            carried = norm_slice(summed, norm_gain, norm_shift, full_width)
            gathered = lax.all_gather(carried, "narrow", axis=1, tiled=True)
        else:
            carried = norm_slice(summed, norm_gain, norm_shift, full_width)
    return (carried, jnp.stack(appended))


def solution(mesh):
    in_specs = (
        P("wide", "narrow"),
        P("wide"),
        P("wide"),
        P(None, None, "wide", "narrow"),
        P("wide", None, "narrow"),
        P(None, "narrow"),
        P("wide", "narrow"),
        P("narrow"),
        P("narrow"),
        P("narrow"),
    )
    out_specs = (P("wide", "narrow"), P(None, None, "wide", "narrow"))
    return jax.shard_map(shards, mesh=mesh, in_specs=in_specs, out_specs=out_specs, check_vma=False)
```

profile of v0, /device:TPU:40, one launch (start us, length us, event | category | flops | bytes accessed | tf_op | source)
XLA Modules:
  0.0 457.5 jit_solution(16025079761975126802)
XLA Ops:
  11.6 2.6 fusion.54
  14.2 1.0 copy.70
  15.3 1.0 copy.51
  16.7 83.8 %all-gather.9.cloned.1.call-done = bf16[2048,3,256]{2,0,1:T(8,128)(2,1)} async-done(((bf16[32,3,256]{2,0,1:T(8,128)(2,1)}), bf16[2048,3,256]{2,0,1:T(8,128)(2,1)}) %all-gather.9.cloned.1.call-update) | async-done | bytes 3145744 | tf_op jit(solution)/shard_map/all_gather | solution.py:95
  100.5 3.2 copy.45
  103.7 41.0 %all-gather.7.cloned.1.call-done = bf16[256,2048]{1,0:T(8,128)(2,1)} async-done(((bf16[256,256]{1,0:T(8,128)(2,1)}), bf16[256,2048]{1,0:T(8,128)(2,1)}) %all-gather.7.cloned.1.call-update) | async-done | bytes 1048592 | tf_op jit(solution)/shard_map/all_gather | solution.py:91
  144.7 2.2 fusion.4
  146.9 0.8 slice_bitcast_fusion.4
  147.7 1.7 copy.68
  149.4 1.2 fusion.55
  150.6 1.8 fusion
  153.4 0.8 convolution_bitcast_fusion.3
  154.3 0.9 fusion.16
  155.3 1.7 copy.54
  157.0 73.5 %all-gather.13.cloned.1.call-done = bf16[2048,256]{1,0:T(8,128)(2,1)} async-done(((bf16[32,256]{1,0:T(8,128)(2,1)}), bf16[2048,256]{1,0:T(8,128)(2,1)}) %all-gather.13.cloned.1.call-update) | async-done | bytes 1048592 | tf_op jit(solution)/shard_map/all_gather | solution.py:113
  230.5 43.9 %all-gather.11.cloned.1.call-done = bf16[256,2048]{0,1:T(8,128)(2,1)} async-done(((bf16[256,256]{0,1:T(8,128)(2,1)}), bf16[256,2048]{0,1:T(8,128)(2,1)}) %all-gather.11.cloned.1.call-update) | async-done | bytes 1048592 | tf_op jit(solution)/shard_map/all_gather | solution.py:112
  274.4 2.8 fusion.56
  277.2 18.7 %psum.28 = f32[256]{0:T(256)S(1)} all-reduce(f32[256]{0:T(256)S(1)} %get-tuple-element.26), channel_id=1, replica_groups=mesh['wide'=64,'narrow'=8] {'narrow'}, use_global_device_ids=true, to_apply=%region_5.6 | all-reduce | flops 256 | bytes 2048 | tf_op jit(solution)/shard_map/psum | solution.py:21
  295.9 1.0 multiply_reduce_fusion.1
  296.9 17.6 %psum.29 = f32[256]{0:T(256)S(1)} all-reduce(f32[256]{0:T(256)S(1)} %multiply_reduce_fusion.1), channel_id=1, replica_groups=mesh['wide'=64,'narrow'=8] {'narrow'}, use_global_device_ids=true, to_apply=%region_7.8 | all-reduce | flops 256 | bytes 2048 | tf_op jit(solution)/shard_map/psum | solution.py:23
  314.5 1.7 add_convert_fusion.1
  316.3 2.0 copy.71
  318.3 2.0 copy.60
  320.4 37.9 %all-gather.15.cloned.1.call-done = bf16[256,2048]{0,1:T(8,128)(2,1)} async-done(((bf16[256,256]{0,1:T(8,128)(2,1)}), bf16[256,2048]{0,1:T(8,128)(2,1)}) %all-gather.15.cloned.1.call-update) | async-done | bytes 1048592 | tf_op jit(solution)/shard_map/all_gather | solution.py:119
  358.2 2.3 fusion.5
  363.2 1.7 copy.69
  365.7 0.9 fusion.17
  366.8 0.8 pad_maximum_fusion
  367.6 43.9 %all-gather.17.cloned.1.call-done = bf16[256,2048]{0,1:T(8,128)(2,1)} async-done(((bf16[256,256]{0,1:T(8,128)(2,1)}), bf16[256,2048]{0,1:T(8,128)(2,1)}) %all-gather.17.cloned.1.call-update) | async-done | bytes 1048592 | tf_op jit(solution)/shard_map/all_gather | solution.py:112
  411.5 1.8 fusion.58
  413.4 18.7 %psum.30 = f32[256]{0:T(256)S(1)} all-reduce(f32[256]{0:T(256)S(1)} %get-tuple-element.32), channel_id=1, replica_groups=mesh['wide'=64,'narrow'=8] {'narrow'}, use_global_device_ids=true, to_apply=%region_13.14 | all-reduce | flops 256 | bytes 2048 | tf_op jit(solution)/shard_map/psum | solution.py:21
  432.1 17.6 %psum.31 = f32[256]{0:T(256)S(1)} all-reduce(f32[256]{0:T(256)S(1)} %multiply_reduce_fusion), channel_id=1, replica_groups=mesh['wide'=64,'narrow'=8] {'narrow'}, use_global_device_ids=true, to_apply=%region_15.16 | all-reduce | flops 256 | bytes 2048 | tf_op jit(solution)/shard_map/psum | solution.py:23
  (71 shorter events, 10.5 us)
Async XLA Ops:
  7.2 93.3 %all-gather.9.cloned.1.call-start = ((), (), s32[]{:S(2)}) async-start(), calls=%async_computation.1 | async-start | bytes 3194880 | tf_op jit(solution)/shard_map/all_gather | solution.py:95
  7.9 136.8 %all-gather.7.cloned.1.call-start = ((), (), s32[]{:S(2)}) async-start(), calls=%async_computation | async-start | bytes 1179648 | tf_op jit(solution)/shard_map/all_gather | solution.py:91
  8.6 221.9 %all-gather.13.cloned.1.call-start = ((), (), s32[]{:S(2)}) async-start(), calls=%async_computation.3 | async-start | bytes 1064960 | tf_op jit(solution)/shard_map/all_gather | solution.py:113
  9.4 265.0 %all-gather.11.cloned.1.call-start = ((), (), s32[]{:S(2)}) async-start(), calls=%async_computation.2 | async-start | bytes 1179648 | tf_op jit(solution)/shard_map/all_gather | solution.py:112
  152.4 1.0 copy-start.2
  153.4 0.9 copy-start.8
  154.3 2.7 copy-start.11
  154.3 2.7 copy-start.12
  154.3 2.7 copy-start.13
  155.3 202.9 %all-gather.15.cloned.1.call-start = ((), (), s32[]{:S(2)}) async-start(), calls=%async_computation.4 | async-start | bytes 1179648 | tf_op jit(solution)/shard_map/all_gather | solution.py:119
  316.2 95.3 %all-gather.17.cloned.1.call-start = ((), (), s32[]{:S(2)}) async-start(), calls=%async_computation.5 | async-start | bytes 1179648 | tf_op jit(solution)/shard_map/all_gather | solution.py:112
  358.2 3.3 copy-start
  362.2 2.6 copy-start.3
  364.8 0.9 copy-start.9
  365.7 1.0 copy-start.4
  365.7 1.0 copy-start.5
  365.7 1.1 copy-start.6
  365.7 1.1 copy-start.7
  365.7 45.8 %copy-start.1 = (bf16[256,256]{0,1:T(8,128)(2,1)S(1)}, bf16[256,256]{0,1:T(8,128)(2,1)}, u32[]{:S(2)}) copy-start(bf16[256,256]{0,1:T(8,128)(2,1)} %add_convert_fusion.1) | copy-start | bytes 393220
  365.7 45.8 %copy-start.10 = (bf16[2048,256]{1,0:T(8,128)(2,1)S(1)}, bf16[2048,256]{1,0:T(8,128)(2,1)}, u32[]{:S(2)}) copy-start(bf16[2048,256]{1,0:T(8,128)(2,1)} %all-gather.13.cloned.1.call-done) | copy-start | bytes 3145732
Sparse Core Ops, SparseCore 0:
  11.4 89.0 all-gather.8
  102.5 42.1 all-gather.6
  148.0 82.4 all-gather.12
  232.4 41.8 all-gather.10
  316.3 41.8 all-gather.14
  366.8 44.6 all-gather.16
where the time goes:
time: 458 us; the launch traced here: 457 us
  waiting for transfers between devices  326 us (71%)
  blocking collectives  72.6 us (16%)
  local copies, waits for them, and re-layouts  20.9 us (5%)
  matrix products  16.5 us (4%)
  between operations  14.4 us (3%)
  other arithmetic  6.96 us (2%)
    all_gather x2, waiting for transfers between devices, shards(): heads_all = lax.all_gather(attended, 'narrow', axis=1, tiled=True)  87.8 us
    all_gather x1, waiting for transfers between devices, shards(): lax.all_gather(w_qkv, 'wide', axis=0, tiled=True)  83.8 us
    all_gather x1, waiting for transfers between devices, shards(): lax.all_gather(w_out, 'wide', axis=0, tiled=True)  73.5 us
    all_gather x1, waiting for transfers between devices, shards(): gathered = lax.all_gather(hidden_in, 'narrow', axis=1, tiled=True)  41 us
    all_gather x1, waiting for transfers between devices, shards(): gathered = lax.all_gather(carried, 'narrow', axis=1, tiled=True)  37.9 us
    psum x2, blocking collectives, norm_slice(): row_means = lax.psum(jnp.sum(values, axis=1), 'narrow') / full_width  37.4 us
    psum x2, blocking collectives, norm_slice(): lax.psum(jnp.sum(centered * centered, axis=1), 'narrow') / full_width  35.2 us
  transfers between devices with their start and end apart: 6, of which 6 were waited for; matrix products, arithmetic and copies ran while one was open for 6% of the time, Pallas kernels for 0%

commit v1 on v0

--- a/solution.py
+++ b/solution.py
@@ -88,7 +88,9 @@
         position[:, None] >= position[None, :]
     )
     bias_flat = qkv_bias.astype(jnp.float32).reshape(-1)
-    gathered = lax.all_gather(hidden_in, "narrow", axis=1, tiled=True)
+    gathered = jnp.concatenate(
+        lax.all_to_all(jnp.stack([hidden_in] * lax.axis_size("narrow")), "narrow", 0, 0), axis=1
+    )
     carried = hidden_in
     appended = []
     for layer_index in range(LAYERS):

time: 458 us -> 410 us (0.90)
  waiting for transfers between devices: 326 us -> 275 us
  starting transfers between devices: 0.24 us -> 5.92 us
    all_gather x1 -> x0, waiting for transfers between devices: 41 us -> none  [shards(): gathered = lax.all_gather(hidden_in, 'narrow', axis=1, tiled=True)]
    all_to_all x0 -> x1, starting transfers between devices: none -> 5.76 us  [shards(): lax.all_to_all(jnp.stack([hidden_in] * lax.axis_size('narrow')), 'narrow'...]
    all_gather x1, waiting for transfers between devices: 73.5 us -> 67.9 us  [shards(): lax.all_gather(w_out, 'wide', axis=0, tiled=True)]
  transfers between devices with their start and end apart: 6 -> 6, of which waited for: 6 -> 5; matrix products, arithmetic and copies ran while one was open for 6% -> 6% of each run, Pallas kernels for 0% -> 0%
where the time goes in v1:
time: 410 us; the launch traced here: 409 us
  waiting for transfers between devices  275 us (67%)
  blocking collectives  72.6 us (18%)
  local copies, waits for them, and re-layouts  18.5 us (5%)
  matrix products  16.6 us (4%)
  between operations  14.1 us (3%)
  other arithmetic  6.3 us (2%)
  starting transfers between devices  5.92 us (1%)
    all_gather x2, waiting for transfers between devices, shards(): heads_all = lax.all_gather(attended, 'narrow', axis=1, tiled=True)  87.9 us
    all_gather x1, waiting for transfers between devices, shards(): lax.all_gather(w_qkv, 'wide', axis=0, tiled=True)  80.2 us
    all_gather x1, waiting for transfers between devices, shards(): lax.all_gather(w_out, 'wide', axis=0, tiled=True)  67.9 us
    all_gather x1, waiting for transfers between devices, shards(): gathered = lax.all_gather(carried, 'narrow', axis=1, tiled=True)  37.8 us
    psum x2, blocking collectives, norm_slice(): row_means = lax.psum(jnp.sum(values, axis=1), 'narrow') / full_width  37.4 us
    psum x2, blocking collectives, norm_slice(): lax.psum(jnp.sum(centered * centered, axis=1), 'narrow') / full_width  35.2 us
    dot_general x4, matrix products, add_rows(): jnp.dot(operand, shard_piece.reshape(piece_rows, -1), preferred_element_t...  9.2 us
  transfers between devices with their start and end apart: 6, of which 5 were waited for; matrix products, arithmetic and copies ran while one was open for 6% of the time, Pallas kernels for 0%

profile of v1, /device:TPU:40, one launch (start us, length us, event | category | flops | bytes accessed | tf_op | source)
XLA Modules:
  0.0 409.2 jit_solution(4333898268683796038)
XLA Ops:
  7.9 1.0 copy.46
  8.9 1.1 stack.38
  10.0 5.8 %all-to-all-start = ((bf16[8,256,256]{1,2,0:T(8,128)(2,1)}), bf16[8,256,256]{1,2,0:T(8,128)(2,1)}, u32[]{:S(2)}, u32[]{:S(2)}) async-start(bf16[8,256,256]{1,2,0:T(8,128)(2,1)} %stack.38), calls=%async_computation | async-start | bytes 2097152 | tf_op jit(solution)/shard_map/all_to_all | solution.py:92
  16.6 1.1 fusion.54
  17.7 1.0 copy.72
  18.7 1.0 copy.53
  20.3 80.2 %all-gather.6.cloned.1.call-done = bf16[2048,3,256]{2,0,1:T(8,128)(2,1)} async-done(((bf16[32,3,256]{2,0,1:T(8,128)(2,1)}), bf16[2048,3,256]{2,0,1:T(8,128)(2,1)}) %all-gather.6.cloned.1.call-update) | async-done | bytes 3145744 | tf_op jit(solution)/shard_map/all_gather | solution.py:97
  100.5 3.2 copy.47
  103.7 2.3 fusion.4
  106.0 0.9 slice_bitcast_fusion.4
  106.8 1.7 copy.70
  108.5 1.2 fusion.55
  109.7 1.8 fusion
  112.5 0.8 convolution_bitcast_fusion.3
  113.4 0.9 fusion.16
  114.5 67.9 %all-gather.10.cloned.1.call-done = bf16[2048,256]{1,0:T(8,128)(2,1)} async-done(((bf16[32,256]{1,0:T(8,128)(2,1)}), bf16[2048,256]{1,0:T(8,128)(2,1)}) %all-gather.10.cloned.1.call-update) | async-done | bytes 1048592 | tf_op jit(solution)/shard_map/all_gather | solution.py:115
  182.4 44.0 %all-gather.8.cloned.1.call-done = bf16[256,2048]{0,1:T(8,128)(2,1)} async-done(((bf16[256,256]{0,1:T(8,128)(2,1)}), bf16[256,2048]{0,1:T(8,128)(2,1)}) %all-gather.8.cloned.1.call-update) | async-done | bytes 1048592 | tf_op jit(solution)/shard_map/all_gather | solution.py:114
  226.4 2.8 fusion.56
  229.2 18.7 %psum.28 = f32[256]{0:T(256)S(1)} all-reduce(f32[256]{0:T(256)S(1)} %get-tuple-element.26), channel_id=1, replica_groups=mesh['wide'=64,'narrow'=8] {'narrow'}, use_global_device_ids=true, to_apply=%region_5.6 | all-reduce | flops 256 | bytes 2048 | tf_op jit(solution)/shard_map/psum | solution.py:21
  247.9 1.0 multiply_reduce_fusion.1
  248.9 17.6 %psum.29 = f32[256]{0:T(256)S(1)} all-reduce(f32[256]{0:T(256)S(1)} %multiply_reduce_fusion.1), channel_id=1, replica_groups=mesh['wide'=64,'narrow'=8] {'narrow'}, use_global_device_ids=true, to_apply=%region_7.8 | all-reduce | flops 256 | bytes 2048 | tf_op jit(solution)/shard_map/psum | solution.py:23
  266.5 1.7 add_convert_fusion.1
  268.3 2.1 copy.73
  270.4 2.0 copy.62
  272.5 37.8 %all-gather.12.cloned.1.call-done = bf16[256,2048]{0,1:T(8,128)(2,1)} async-done(((bf16[256,256]{0,1:T(8,128)(2,1)}), bf16[256,2048]{0,1:T(8,128)(2,1)}) %all-gather.12.cloned.1.call-update) | async-done | bytes 1048592 | tf_op jit(solution)/shard_map/all_gather | solution.py:121
  310.3 2.3 fusion.5
  315.2 1.7 copy.71
  317.8 0.9 fusion.17
  319.7 43.9 %all-gather.14.cloned.1.call-done = bf16[256,2048]{0,1:T(8,128)(2,1)} async-done(((bf16[256,256]{0,1:T(8,128)(2,1)}), bf16[256,2048]{0,1:T(8,128)(2,1)}) %all-gather.14.cloned.1.call-update) | async-done | bytes 1048592 | tf_op jit(solution)/shard_map/all_gather | solution.py:114
  363.6 1.8 fusion.58
  365.4 18.7 %psum.30 = f32[256]{0:T(256)S(1)} all-reduce(f32[256]{0:T(256)S(1)} %get-tuple-element.32), channel_id=1, replica_groups=mesh['wide'=64,'narrow'=8] {'narrow'}, use_global_device_ids=true, to_apply=%region_13.14 | all-reduce | flops 256 | bytes 2048 | tf_op jit(solution)/shard_map/psum | solution.py:21
  384.2 17.6 %psum.31 = f32[256]{0:T(256)S(1)} all-reduce(f32[256]{0:T(256)S(1)} %multiply_reduce_fusion), channel_id=1, replica_groups=mesh['wide'=64,'narrow'=8] {'narrow'}, use_global_device_ids=true, to_apply=%region_15.16 | all-reduce | flops 256 | bytes 2048 | tf_op jit(solution)/shard_map/psum | solution.py:23
  (81 shorter events, 8.7 us)
Async XLA Ops:
  7.2 9.4 %copy-start.12 = (bf16[3,256]{1,0:T(4,128)(2,1)S(1)}, bf16[3,256]{1,0:T(4,128)(2,1)}, u32[]{:S(2)}) copy-start(bf16[3,256]{1,0:T(4,128)(2,1)} %param.15) | copy-start | bytes 4612
  7.2 9.4 %copy-start.1 = (bf16[2,2,1024,256]{3,2,1,0:T(8,128)(2,1)S(1)}, bf16[2,2,1024,256]{3,2,1,0:T(8,128)(2,1)}, u32[]{:S(2)}) copy-start(bf16[2,2,1024,256]{3,2,1,0:T(8,128)(2,1)} %param.13) | copy-start | bytes 6291460
  7.2 93.3 %all-gather.6.cloned.1.call-start = ((), (), s32[]{:S(2)}) async-start(), calls=%async_computation.1 | async-start | bytes 3194880 | tf_op jit(solution)/shard_map/all_gather | solution.py:97
  8.9 7.7 %copy-start.2 = (bf16[256,256]{0,1:T(8,128)(2,1)}, bf16[256,256]{0,1:T(8,128)(2,1)S(1)}, u32[]{:S(2)}) copy-start(bf16[256,256]{0,1:T(8,128)(2,1)S(1)} %copy.46) | copy-start | bytes 393220
  10.0 93.7 %all-to-all-start = ((bf16[8,256,256]{1,2,0:T(8,128)(2,1)}), bf16[8,256,256]{1,2,0:T(8,128)(2,1)}, u32[]{:S(2)}, u32[]{:S(2)}) async-start(bf16[8,256,256]{1,2,0:T(8,128)(2,1)} %stack.38), calls=%async_computation | async-start | bytes 2097152 | tf_op jit(solution)/shard_map/all_to_all | solution.py:92
  15.8 166.6 %all-gather.10.cloned.1.call-start = ((), (), s32[]{:S(2)}) async-start(), calls=%async_computation.3 | async-start | bytes 1064960 | tf_op jit(solution)/shard_map/all_gather | solution.py:115
  16.5 209.9 %all-gather.8.cloned.1.call-start = ((), (), s32[]{:S(2)}) async-start(), calls=%async_computation.2 | async-start | bytes 1179648 | tf_op jit(solution)/shard_map/all_gather | solution.py:114
  17.7 2.0 copy-start.14
  17.7 2.1 copy-start.13
  111.5 1.0 copy-start.4
  112.5 0.9 copy-start.10
  113.4 1.1 copy-start.16
  113.4 1.1 copy-start.17
  113.4 1.1 copy-start.18
  114.4 195.9 %all-gather.12.cloned.1.call-start = ((), (), s32[]{:S(2)}) async-start(), calls=%async_computation.4 | async-start | bytes 1179648 | tf_op jit(solution)/shard_map/all_gather | solution.py:121
  268.3 95.3 %all-gather.14.cloned.1.call-start = ((), (), s32[]{:S(2)}) async-start(), calls=%async_computation.5 | async-start | bytes 1179648 | tf_op jit(solution)/shard_map/all_gather | solution.py:114
  310.3 3.3 copy-start
  314.3 2.6 copy-start.5
  316.9 0.9 copy-start.11
  317.7 1.0 copy-start.6
  317.7 1.0 copy-start.7
  317.7 1.1 copy-start.8
  317.8 1.1 copy-start.9
  317.8 45.8 %copy-start.3 = (bf16[256,256]{0,1:T(8,128)(2,1)S(1)}, bf16[256,256]{0,1:T(8,128)(2,1)}, u32[]{:S(2)}) copy-start(bf16[256,256]{0,1:T(8,128)(2,1)} %add_convert_fusion.1) | copy-start | bytes 393220
  317.8 45.8 %copy-start.15 = (bf16[2048,256]{1,0:T(8,128)(2,1)S(1)}, bf16[2048,256]{1,0:T(8,128)(2,1)}, u32[]{:S(2)}) copy-start(bf16[2048,256]{1,0:T(8,128)(2,1)} %all-gather.10.cloned.1.call-done) | copy-start | bytes 3145732
Sparse Core Ops, SparseCore 0:
  11.4 89.0 all-gather.5
  103.9 78.4 all-gather.9
  184.5 41.8 all-gather.7
  268.4 41.8 all-gather.11
  318.9 44.6 all-gather.13
